TPU v7x, 32 devices: a whole 2x2x4 slice. The times are simulated.
32 devices in a mesh: seq: 8 (over y, x, core), dp: 4 (over z).
Axes of the slice: x: 2, y: 2, z: 4, core: 2. Of those that a mesh axis runs over, the one named last changes fastest.
Arguments:
- query: bfloat16 [4, 1536, 1280], P('dp', 'seq'), may hold values from -52 to 52, as said below
- keys: bfloat16 [4, 1536, 1280], P('dp', 'seq'), may hold values from -6 to 6, as said below
- values: bfloat16 [4, 1536, 1280], P('dp', 'seq'), may hold values from -6 to 6
- attn: bfloat16 [4, 1536, 1280], P('dp', 'seq'), may hold values from -6 to 6
- d_block: bfloat16 [4, 1536, 1280], P('dp', 'seq'), may hold values from -6 to 6
- w_out: bfloat16 [1280, 1280], P('dp'), may hold values from -0.15625 to 0.15625
Outputs:
- d_query: bfloat16 [4, 1536, 1280], P('dp', 'seq')
- d_keys: bfloat16 [4, 1536, 1280], P('dp', 'seq')
- d_values: bfloat16 [4, 1536, 1280], P('dp', 'seq')
- d_weight: float32 [1280, 1280], P('dp')
Inputs may be any that keep to these rules, and one draw needn't show every extreme that they name: Some query patches may lie along the sum of two keys of the same video. keys has entries of order one.
All inputs are finite; a program needn't handle non-finite values.
Results may differ from a plain program's by a relative error of at most 0.0058.
Values may be sent and summed in bfloat16 or wider, within the bound.
A program may use at most 64 MiB of HBM per device.

v0:
```python
import jax
import jax.numpy as jnp
from jax import lax
from jax.sharding import PartitionSpec as P

HEAD_DIM = 80


def head_backward(query_h, keys_h, values_h, dout_h, delta_h):
    patch_total = query_h.shape[0]
    block_rows = min(512, patch_total)
    while patch_total % block_rows != 0:
        block_rows = block_rows // 2
    block_total = patch_total // block_rows
    score_scale = HEAD_DIM ** (-0.5)
    contract_last = (((1,), (1,)), ((), ()))
    contract_first = (((0,), (0,)), ((), ()))

    def one_block(carry, inputs):
        keys_grad, values_grad = carry
        query_block, dout_block, delta_block = inputs
        scores = (
            lax.dot_general(query_block, keys_h, contract_last, preferred_element_type=jnp.float32)
            * score_scale
        )
        row_max = jnp.max(scores, axis=1, keepdims=True)
        lse = row_max + jnp.log(jnp.sum(jnp.exp(scores - row_max), axis=1, keepdims=True))
        probs = jnp.exp(scores - lse)
        probs_low = probs.astype(jnp.bfloat16)
        values_grad = values_grad + lax.dot_general(
            probs_low, dout_block, contract_first, preferred_element_type=jnp.float32
        )
        d_probs = lax.dot_general(
            dout_block, values_h, contract_last, preferred_element_type=jnp.float32
        )
        d_scores = (score_scale * probs * (d_probs - delta_block[:, None])).astype(jnp.bfloat16)
        query_grad = jnp.dot(d_scores, keys_h, preferred_element_type=jnp.float32)
        keys_grad = keys_grad + lax.dot_general(
            d_scores, query_block, contract_first, preferred_element_type=jnp.float32
        )
        return ((keys_grad, values_grad), query_grad.astype(jnp.bfloat16))

    empty = jnp.zeros((patch_total, HEAD_DIM), jnp.float32)
    blocked = (
        query_h.reshape(block_total, block_rows, HEAD_DIM),
        dout_h.reshape(block_total, block_rows, HEAD_DIM),
        delta_h.reshape(block_total, block_rows),
    )
    (keys_grad, values_grad), query_blocks = lax.scan(one_block, (empty, empty), blocked)
    return (
        query_blocks.reshape(patch_total, HEAD_DIM),
        keys_grad.astype(jnp.bfloat16),
        values_grad.astype(jnp.bfloat16),
    )


def body(query, keys, values, attn, d_block, w_out):
    seq_count = lax.axis_size("seq")
    dp_count = lax.axis_size("dp")
    tok_rows = query.shape[1]
    features = query.shape[2]
    head_here = features // HEAD_DIM // seq_count
    grad_y = d_block.reshape(tok_rows, features)
    attn_rows = attn.reshape(tok_rows, features)
    d_out = lax.dot_general(
        grad_y,
        lax.all_gather(w_out, "dp", axis=0, tiled=True),
        (((1,), (1,)), ((), ())),
        preferred_element_type=jnp.float32,
    ).astype(jnp.bfloat16)

    def split_heads(array):
        return array.reshape(tok_rows, seq_count, head_here, HEAD_DIM)

    query_all, keys_all, values_all, dout_all, output_all = (
        lax.all_to_all(split_heads(query), "seq", split_axis=1, concat_axis=0, tiled=True),
        lax.all_to_all(split_heads(keys), "seq", split_axis=1, concat_axis=0, tiled=True),
        lax.all_to_all(split_heads(values), "seq", split_axis=1, concat_axis=0, tiled=True),
        lax.all_to_all(split_heads(d_out), "seq", split_axis=1, concat_axis=0, tiled=True),
        lax.all_to_all(split_heads(attn_rows), "seq", split_axis=1, concat_axis=0, tiled=True),
    )
    row_terms = jnp.sum(dout_all.astype(jnp.float32) * output_all.astype(jnp.float32), axis=3)
    query_list = []
    keys_list = []
    values_list = []
    for head in range(head_here):
        gradient = head_backward(
            query_all[:, 0, head],
            keys_all[:, 0, head],
            values_all[:, 0, head],
            dout_all[:, 0, head],
            row_terms[:, 0, head],
        )
        query_list.append(gradient[0])
        keys_list.append(gradient[1])
        values_list.append(gradient[2])
    query_heads = jnp.stack(query_list, axis=1)[:, None]
    keys_heads = jnp.stack(keys_list, axis=1)[:, None]
    values_heads = jnp.stack(values_list, axis=1)[:, None]
    query_back, keys_back, values_back = (
        lax.all_to_all(query_heads, "seq", split_axis=0, concat_axis=1, tiled=True),
        lax.all_to_all(keys_heads, "seq", split_axis=0, concat_axis=1, tiled=True),
        lax.all_to_all(values_heads, "seq", split_axis=0, concat_axis=1, tiled=True),
    )
    factor = 1.0 / float(dp_count * tok_rows * seq_count) ** 0.5
    contract_first = (((0,), (0,)), ((), ()))
    partial_rows = lax.psum_scatter(
        lax.dot_general(attn_rows, grad_y, contract_first, preferred_element_type=jnp.float32)
        * factor,
        "dp",
        scatter_dimension=0,
        tiled=True,
    )
    d_weight = lax.psum(partial_rows, "seq")
    shape_out = (1, tok_rows, features)
    return (
        query_back.reshape(shape_out),
        keys_back.reshape(shape_out),
        values_back.reshape(shape_out),
        d_weight,
    )


def solution(mesh):
    return jax.shard_map(
        body,
        mesh=mesh,
        in_specs=(
            P("dp", "seq", None),
            P("dp", "seq", None),
            P("dp", "seq", None),
            P("dp", "seq", None),
            P("dp", "seq", None),
            P("dp", None),
        ),
        out_specs=(P("dp", "seq", None), P("dp", "seq", None), P("dp", "seq", None), P("dp", None)),
        check_vma=False,
    )
```

profile of v0, /device:TPU:0, one launch (start us, length us, event | category | flops | bytes accessed | tf_op | source)
XLA Modules:
  0.0 278.9 jit_solution(8899856098852248446)
XLA Ops:
  10.0 5.2 %all-to-all-start = ((bf16[192,8,2,80]{0,3,2,1:T(8,128)(2,1)}), bf16[192,8,2,80]{0,3,2,1:T(8,128)(2,1)S(1)}, u32[]{:S(2)}, u32[]{:S(2)}) async-start(bf16[192,8,2,80]{0,3,2,1:T(8,128)(2,1)} %bitcast), calls=%async_computation | async-start | bytes 1310720 | tf_op jit(solution)/shard_map/all_to_all | solution.py:76
  15.3 3.8 %convolution_multiply_fusion.2 = f32[1280,1280]{1,0:T(8,128)} fusion(bf16[1,192,1280]{2,1,0:T(8,128)(2,1)S(1)} %copy-done.8, bf16[1,192,1280]{2,1,0:T(8,128)(2,1)S(1)} %copy-done), kind=kOutput, calls=%fused_computation.54 | convolution fusion | flops 630784000 | bytes 7536640 | tf_op jit(solution)/shard_map/dot_general | solution.py:108
  26.3 4.2 %all-to-all-start.1 = ((bf16[192,8,2,80]{0,3,2,1:T(8,128)(2,1)}), bf16[192,8,2,80]{0,3,2,1:T(8,128)(2,1)}, u32[]{:S(2)}, u32[]{:S(2)}) async-start(bf16[192,8,2,80]{0,3,2,1:T(8,128)(2,1)} %bitcast.192), calls=%async_computation.1 | async-start | bytes 1310720 | tf_op jit(solution)/shard_map/all_to_all | solution.py:77
  34.5 7.2 %all-to-all-done.1 = bf16[192,8,2,80]{0,3,2,1:T(8,128)(2,1)} async-done(((bf16[192,8,2,80]{0,3,2,1:T(8,128)(2,1)}), bf16[192,8,2,80]{0,3,2,1:T(8,128)(2,1)}, u32[]{:S(2)}, u32[]{:S(2)}) %all-to-all-start.1) | async-done | bytes 491552 | tf_op jit(solution)/shard_map/all_to_all | solution.py:77
  41.7 4.2 %all-to-all-start.3 = ((bf16[192,8,2,80]{0,3,2,1:T(8,128)(2,1)}), bf16[192,8,2,80]{0,3,2,1:T(8,128)(2,1)}, u32[]{:S(2)}, u32[]{:S(2)}) async-start(bf16[192,8,2,80]{0,3,2,1:T(8,128)(2,1)} %bitcast.13), calls=%async_computation.3 | async-start | bytes 1310720 | tf_op jit(solution)/shard_map/all_to_all | solution.py:78
  50.7 6.4 %all-to-all-done.3 = bf16[192,8,2,80]{0,3,2,1:T(8,128)(2,1)} async-done(((bf16[192,8,2,80]{0,3,2,1:T(8,128)(2,1)}), bf16[192,8,2,80]{0,3,2,1:T(8,128)(2,1)}, u32[]{:S(2)}, u32[]{:S(2)}) %all-to-all-start.3) | async-done | bytes 491552 | tf_op jit(solution)/shard_map/all_to_all | solution.py:78
  61.7 16.2 %all-gather.2.cloned.1.call-done = bf16[1280,1280]{1,0:T(8,128)(2,1)} async-done(((bf16[320,1280]{1,0:T(8,128)(2,1)}), bf16[1280,1280]{1,0:T(8,128)(2,1)}) %all-gather.2.cloned.1.call-update) | async-done | bytes 3276816 | tf_op jit(solution)/shard_map/all_gather | solution.py:67
  77.9 3.9 %convolution_convert_fusion.2 = bf16[192,1280]{1,0:T(8,128)(2,1)} fusion(bf16[1280,1280]{1,0:T(8,128)(2,1)} %all-gather.2.cloned.1.call-done, bf16[1,192,1280]{2,1,0:T(8,128)(2,1)S(1)} %copy-done), kind=kOutput, calls=%fused_computation.55 | convolution fusion | flops 629391360 | bytes 4259840 | tf_op jit(solution)/shard_map/dot_general | solution.py:65
  84.0 4.2 %all-to-all-start.2 = ((bf16[192,8,2,80]{0,3,2,1:T(8,128)(2,1)}), bf16[192,8,2,80]{0,3,2,1:T(8,128)(2,1)}, u32[]{:S(2)}, u32[]{:S(2)}) async-start(bf16[192,8,2,80]{0,3,2,1:T(8,128)(2,1)} %bitcast.193), calls=%async_computation.2 | async-start | bytes 1310720 | tf_op jit(solution)/shard_map/all_to_all | solution.py:79
  94.9 4.5 %all-to-all-done.2 = bf16[192,8,2,80]{0,3,2,1:T(8,128)(2,1)} async-done(((bf16[192,8,2,80]{0,3,2,1:T(8,128)(2,1)}), bf16[192,8,2,80]{0,3,2,1:T(8,128)(2,1)}, u32[]{:S(2)}, u32[]{:S(2)}) %all-to-all-start.2) | async-done | bytes 491552 | tf_op jit(solution)/shard_map/all_to_all | solution.py:79
  99.3 4.4 %all-to-all-start.4 = ((bf16[192,8,2,80]{0,3,2,1:T(8,128)(2,1)}), bf16[192,8,2,80]{0,3,2,1:T(8,128)(2,1)}, u32[]{:S(2)}, u32[]{:S(2)}) async-start(bf16[192,8,2,80]{0,3,2,1:T(8,128)(2,1)} %bitcast.190), calls=%async_computation.4 | async-start | bytes 1310720 | tf_op jit(solution)/shard_map/all_to_all | solution.py:80
  117.4 31.8 %while.30 = (s32[]{:T(128)}, f32[1536,80]{0,1:T(8,128)S(1)}, f32[1536,80]{0,1:T(8,128)S(1)}, bf16[3,512,80]{1,2,0:T(8,128)(2,1)S(1)}, bf16[3,512,80]{2,1,0:T(8,1...) while((s32[]{:T(128)}, f32[1536,80]{0,1:T(8,128)S(1)}, ...), condition=%wide.region_4.5_spmd.clone, body=%wide.region_1.4_spmd.clone.sunk | while | flops 638328320 | bytes 46932176 | solution.py:49
  121.3 2.8 %convolution_add_fusion.9 = f32[1536,80]{0,1:T(8,128)S(1)} fusion(f32[512,1536]{1,0:T(8,128)} %copy-done.1, f32[512]{0:T(512)S(1)} %log_add_fusion.4, f32[1536,80]{0,1:T(8,128)S(1)} %get-tuple-element.496, pred[]{:T(512)S(6)} %compare.6, bf16[3,512,80]{2,1,0:T(8,128)(2,1)} %get-tuple-element.511, s32[]{:T(128)} %get-tuple-element.494), kind=kOutput, calls=%fused_computation.7.clone.1 | convolution fusion | flops 127647744 | bytes 4262401 | tf_op jit(solution)/shard_map/while/body/eval_jaxpr/dot_general | solution.py:30
  131.9 2.8 %convolution_add_fusion.9 = f32[1536,80]{0,1:T(8,128)S(1)} fusion(f32[512,1536]{1,0:T(8,128)} %copy-done.1, f32[512]{0:T(512)S(1)} %log_add_fusion.4, f32[1536,80]{0,1:T(8,128)S(1)} %get-tuple-element.496, pred[]{:T(512)S(6)} %compare.6, bf16[3,512,80]{2,1,0:T(8,128)(2,1)} %get-tuple-element.511, s32[]{:T(128)} %get-tuple-element.494), kind=kOutput, calls=%fused_computation.7.clone.1 | convolution fusion | flops 127647744 | bytes 4262401 | tf_op jit(solution)/shard_map/while/body/eval_jaxpr/dot_general | solution.py:30
  142.5 2.8 %convolution_add_fusion.9 = f32[1536,80]{0,1:T(8,128)S(1)} fusion(f32[512,1536]{1,0:T(8,128)} %copy-done.1, f32[512]{0:T(512)S(1)} %log_add_fusion.4, f32[1536,80]{0,1:T(8,128)S(1)} %get-tuple-element.496, pred[]{:T(512)S(6)} %compare.6, bf16[3,512,80]{2,1,0:T(8,128)(2,1)} %get-tuple-element.511, s32[]{:T(128)} %get-tuple-element.494), kind=kOutput, calls=%fused_computation.7.clone.1 | convolution fusion | flops 127647744 | bytes 4262401 | tf_op jit(solution)/shard_map/while/body/eval_jaxpr/dot_general | solution.py:30
  150.0 29.2 %while.31 = (s32[]{:T(128)}, f32[1536,80]{0,1:T(8,128)S(1)}, f32[1536,80]{0,1:T(8,128)S(1)}, bf16[3,512,80]{1,2,0:T(8,128)(2,1)S(1)}, bf16[3,512,80]{2,1,0:T(8,1...) while((s32[]{:T(128)}, f32[1536,80]{0,1:T(8,128)S(1)}, ...), condition=%wide.region_8.9_spmd.clone, body=%wide.region_5.8_spmd.clone.sunk | while | flops 638328320 | bytes 48061684 | solution.py:49
  163.8 2.8 %convolution_add_fusion.11 = f32[1536,80]{0,1:T(8,128)S(1)} fusion(f32[512,1536]{1,0:T(8,128)} %copy-done.3, f32[512]{0:T(512)S(1)} %log_add_fusion.5, f32[1536,80]{0,1:T(8,128)S(1)} %get-tuple-element.463, pred[]{:T(512)S(6)} %compare.7, bf16[3,512,80]{2,1,0:T(8,128)(2,1)S(1)} %copy-done.7, s32[]{:T(128)} %get-tuple-element.461), kind=kOutput, calls=%fused_computation.34.clone.1 | convolution fusion | flops 127647744 | bytes 4261893 | tf_op jit(solution)/shard_map/while/body/eval_jaxpr/dot_general | solution.py:30
  182.1 3.5 %all-to-all-start.7 = ((bf16[1536,1,2,80]{3,2,1,0:T(2,128)(2,1)}), bf16[1536,1,2,80]{3,2,1,0:T(2,128)(2,1)S(1)}, u32[]{:S(2)}, u32[]{:S(2)}) async-start(bf16[1536,1,2,80]{3,2,1,0:T(2,128)(2,1)} %copy.137), calls=%async_computation.7 | async-start | bytes 1572864 | tf_op jit(solution)/shard_map/all_to_all | solution.py:103
  187.6 10.6 %all-to-all-done.7 = bf16[1536,1,2,80]{3,2,1,0:T(2,128)(2,1)S(1)} async-done(((bf16[1536,1,2,80]{3,2,1,0:T(2,128)(2,1)}), bf16[1536,1,2,80]{3,2,1,0:T(2,128)(2,1)S(1)}, u32[]{:S(2)}, u32[]{:S(2)}) %all-to-all-start.7) | async-done | bytes 491552 | tf_op jit(solution)/shard_map/all_to_all | solution.py:103
  198.2 3.5 %all-to-all-start.6 = ((bf16[1536,1,2,80]{3,2,1,0:T(2,128)(2,1)}), bf16[1536,1,2,80]{3,2,1,0:T(2,128)(2,1)S(1)}, u32[]{:S(2)}, u32[]{:S(2)}) async-start(bf16[1536,1,2,80]{3,2,1,0:T(2,128)(2,1)} %copy.135), calls=%async_computation.6 | async-start | bytes 1572864 | tf_op jit(solution)/shard_map/all_to_all | solution.py:102
  205.5 10.5 %all-to-all-done.6 = bf16[1536,1,2,80]{3,2,1,0:T(2,128)(2,1)S(1)} async-done(((bf16[1536,1,2,80]{3,2,1,0:T(2,128)(2,1)}), bf16[1536,1,2,80]{3,2,1,0:T(2,128)(2,1)S(1)}, u32[]{:S(2)}, u32[]{:S(2)}) %all-to-all-start.6) | async-done | bytes 491552 | tf_op jit(solution)/shard_map/all_to_all | solution.py:102
  215.9 3.6 %all-to-all-start.5 = ((bf16[1536,1,2,80]{3,2,1,0:T(2,128)(2,1)}), bf16[1536,1,2,80]{3,2,1,0:T(2,128)(2,1)S(1)}, u32[]{:S(2)}, u32[]{:S(2)}) async-start(bf16[1536,1,2,80]{3,2,1,0:T(2,128)(2,1)} %copy.132), calls=%async_computation.5 | async-start | bytes 1572864 | tf_op jit(solution)/shard_map/all_to_all | solution.py:101
  225.7 6.2 %all-to-all-done.5 = bf16[1536,1,2,80]{3,2,1,0:T(2,128)(2,1)S(1)} async-done(((bf16[1536,1,2,80]{3,2,1,0:T(2,128)(2,1)}), bf16[1536,1,2,80]{3,2,1,0:T(2,128)(2,1)S(1)}, u32[]{:S(2)}, u32[]{:S(2)}) %all-to-all-start.5) | async-done | bytes 491552 | tf_op jit(solution)/shard_map/all_to_all | solution.py:101
  233.9 35.8 %all-reduce.2.cloned.1.call-done = f32[320,1280]{1,0:T(8,128)} async-done(((f32[320,1280]{1,0:T(8,128)}), f32[320,1280]{1,0:T(8,128)}) %all-reduce.2.cloned.1.call-update) | async-done | bytes 1638416 | tf_op jit(solution)/shard_map/psum | solution.py:114
  (158 shorter events, 115.1 us)
Async XLA Ops:
  7.2 8.1 %copy-start = (bf16[1,192,1280]{2,1,0:T(8,128)(2,1)S(1)}, bf16[1,192,1280]{2,1,0:T(8,128)(2,1)}, u32[]{:S(2)}) copy-start(bf16[1,192,1280]{2,1,0:T(8,128)(2,1)} %param.14) | copy-start | bytes 1474564
  7.2 8.1 %copy-start.8 = (bf16[1,192,1280]{2,1,0:T(8,128)(2,1)S(1)}, bf16[1,192,1280]{2,1,0:T(8,128)(2,1)}, u32[]{:S(2)}) copy-start(bf16[1,192,1280]{2,1,0:T(8,128)(2,1)} %param.13) | copy-start | bytes 1474564
  7.2 70.7 %all-gather.2.cloned.1.call-start = ((), (), s32[]{:S(2)}) async-start(), calls=%async_computation.9 | async-start | bytes 4096000 | tf_op jit(solution)/shard_map/all_gather | solution.py:67
  10.0 16.3 %all-to-all-start = ((bf16[192,8,2,80]{0,3,2,1:T(8,128)(2,1)}), bf16[192,8,2,80]{0,3,2,1:T(8,128)(2,1)S(1)}, u32[]{:S(2)}, u32[]{:S(2)}) async-start(bf16[192,8,2,80]{0,3,2,1:T(8,128)(2,1)} %bitcast), calls=%async_computation | async-start | bytes 1310720 | tf_op jit(solution)/shard_map/all_to_all | solution.py:76
  15.2 186.6 %reduce-scatter.2.cloned.1.call-start = ((), (), s32[]{:S(2)}) async-start(), calls=%async_computation.10 | async-start | bytes 8192000 | tf_op jit(solution)/shard_map/reduce_scatter | solution.py:107
  26.3 15.3 %all-to-all-start.1 = ((bf16[192,8,2,80]{0,3,2,1:T(8,128)(2,1)}), bf16[192,8,2,80]{0,3,2,1:T(8,128)(2,1)}, u32[]{:S(2)}, u32[]{:S(2)}) async-start(bf16[192,8,2,80]{0,3,2,1:T(8,128)(2,1)} %bitcast.192), calls=%async_computation.1 | async-start | bytes 1310720 | tf_op jit(solution)/shard_map/all_to_all | solution.py:77
  41.7 15.3 %all-to-all-start.3 = ((bf16[192,8,2,80]{0,3,2,1:T(8,128)(2,1)}), bf16[192,8,2,80]{0,3,2,1:T(8,128)(2,1)}, u32[]{:S(2)}, u32[]{:S(2)}) async-start(bf16[192,8,2,80]{0,3,2,1:T(8,128)(2,1)} %bitcast.13), calls=%async_computation.3 | async-start | bytes 1310720 | tf_op jit(solution)/shard_map/all_to_all | solution.py:78
  84.0 15.4 %all-to-all-start.2 = ((bf16[192,8,2,80]{0,3,2,1:T(8,128)(2,1)}), bf16[192,8,2,80]{0,3,2,1:T(8,128)(2,1)}, u32[]{:S(2)}, u32[]{:S(2)}) async-start(bf16[192,8,2,80]{0,3,2,1:T(8,128)(2,1)} %bitcast.193), calls=%async_computation.2 | async-start | bytes 1310720 | tf_op jit(solution)/shard_map/all_to_all | solution.py:79
  99.3 15.3 %all-to-all-start.4 = ((bf16[192,8,2,80]{0,3,2,1:T(8,128)(2,1)}), bf16[192,8,2,80]{0,3,2,1:T(8,128)(2,1)}, u32[]{:S(2)}, u32[]{:S(2)}) async-start(bf16[192,8,2,80]{0,3,2,1:T(8,128)(2,1)} %bitcast.190), calls=%async_computation.4 | async-start | bytes 1310720 | tf_op jit(solution)/shard_map/all_to_all | solution.py:80
  121.2 2.9 %copy-start.6 = (bf16[1536,80]{1,0:T(8,128)(2,1)S(1)}, bf16[1536,80]{1,0:T(8,128)(2,1)}, u32[]{:S(2)}) copy-start(bf16[1536,80]{1,0:T(8,128)(2,1)} %get-tuple-element.512) | copy-start | bytes 737284 | tf_op jit(solution)/shard_map/while
  131.8 2.9 %copy-start.6 = (bf16[1536,80]{1,0:T(8,128)(2,1)S(1)}, bf16[1536,80]{1,0:T(8,128)(2,1)}, u32[]{:S(2)}) copy-start(bf16[1536,80]{1,0:T(8,128)(2,1)} %get-tuple-element.512) | copy-start | bytes 737284 | tf_op jit(solution)/shard_map/while
  142.5 2.9 %copy-start.6 = (bf16[1536,80]{1,0:T(8,128)(2,1)S(1)}, bf16[1536,80]{1,0:T(8,128)(2,1)}, u32[]{:S(2)}) copy-start(bf16[1536,80]{1,0:T(8,128)(2,1)} %get-tuple-element.512) | copy-start | bytes 737284 | tf_op jit(solution)/shard_map/while
  150.0 3.9 %copy-start.7 = (bf16[3,512,80]{2,1,0:T(8,128)(2,1)S(1)}, bf16[3,512,80]{2,1,0:T(8,128)(2,1)}, u32[]{:S(2)}) copy-start(bf16[3,512,80]{2,1,0:T(8,128)(2,1)} %get-tuple-element.478) | copy-start | bytes 737284 | tf_op jit(solution)/shard_map/while
  153.4 3.5 %copy-start.5 = (bf16[1536,80]{1,0:T(8,128)(2,1)S(1)}, bf16[1536,80]{1,0:T(8,128)(2,1)}, u32[]{:S(2)}) copy-start(bf16[1536,80]{1,0:T(8,128)(2,1)} %get-tuple-element.479) | copy-start | bytes 737284 | tf_op jit(solution)/shard_map/while
  154.0 3.0 %copy-start.4 = (f32[512,1536]{1,0:T(8,128)S(1)}, f32[512,1536]{1,0:T(8,128)}, u32[]{:S(2)}) copy-start(f32[512,1536]{1,0:T(8,128)} %copy-done.3) | copy-start | bytes 9437188 | tf_op jit(solution)/shard_map/while
  159.8 4.0 %copy-start.7 = (bf16[3,512,80]{2,1,0:T(8,128)(2,1)S(1)}, bf16[3,512,80]{2,1,0:T(8,128)(2,1)}, u32[]{:S(2)}) copy-start(bf16[3,512,80]{2,1,0:T(8,128)(2,1)} %get-tuple-element.478) | copy-start | bytes 737284 | tf_op jit(solution)/shard_map/while
  163.2 3.5 %copy-start.5 = (bf16[1536,80]{1,0:T(8,128)(2,1)S(1)}, bf16[1536,80]{1,0:T(8,128)(2,1)}, u32[]{:S(2)}) copy-start(bf16[1536,80]{1,0:T(8,128)(2,1)} %get-tuple-element.479) | copy-start | bytes 737284 | tf_op jit(solution)/shard_map/while
  169.5 3.9 %copy-start.7 = (bf16[3,512,80]{2,1,0:T(8,128)(2,1)S(1)}, bf16[3,512,80]{2,1,0:T(8,128)(2,1)}, u32[]{:S(2)}) copy-start(bf16[3,512,80]{2,1,0:T(8,128)(2,1)} %get-tuple-element.478) | copy-start | bytes 737284 | tf_op jit(solution)/shard_map/while
  172.9 3.5 %copy-start.5 = (bf16[1536,80]{1,0:T(8,128)(2,1)S(1)}, bf16[1536,80]{1,0:T(8,128)(2,1)}, u32[]{:S(2)}) copy-start(bf16[1536,80]{1,0:T(8,128)(2,1)} %get-tuple-element.479) | copy-start | bytes 737284 | tf_op jit(solution)/shard_map/while
  179.2 6.5 %copy-start.9 = (bf16[1536,1,80]{0,2,1:T(8,128)(2,1)S(1)}, bf16[1536,1,80]{0,2,1:T(8,128)(2,1)}, u32[]{:S(2)}) copy-start(bf16[1536,1,80]{0,2,1:T(8,128)(2,1)} %get-tuple-element.331) | copy-start | bytes 737284
  182.1 16.1 %all-to-all-start.7 = ((bf16[1536,1,2,80]{3,2,1,0:T(2,128)(2,1)}), bf16[1536,1,2,80]{3,2,1,0:T(2,128)(2,1)S(1)}, u32[]{:S(2)}, u32[]{:S(2)}) async-start(bf16[1536,1,2,80]{3,2,1,0:T(2,128)(2,1)} %copy.137), calls=%async_computation.7 | async-start | bytes 1572864 | tf_op jit(solution)/shard_map/all_to_all | solution.py:103
  198.2 17.7 %all-to-all-start.6 = ((bf16[1536,1,2,80]{3,2,1,0:T(2,128)(2,1)}), bf16[1536,1,2,80]{3,2,1,0:T(2,128)(2,1)S(1)}, u32[]{:S(2)}, u32[]{:S(2)}) async-start(bf16[1536,1,2,80]{3,2,1,0:T(2,128)(2,1)} %copy.135), calls=%async_computation.6 | async-start | bytes 1572864 | tf_op jit(solution)/shard_map/all_to_all | solution.py:102
  201.8 67.9 %all-reduce.2.cloned.1.call-start = ((), (), s32[]{:S(2)}) async-start(), calls=%async_computation.11 | async-start | bytes 3276800 | tf_op jit(solution)/shard_map/psum | solution.py:114
  215.9 16.1 %all-to-all-start.5 = ((bf16[1536,1,2,80]{3,2,1,0:T(2,128)(2,1)}), bf16[1536,1,2,80]{3,2,1,0:T(2,128)(2,1)S(1)}, u32[]{:S(2)}, u32[]{:S(2)}) async-start(bf16[1536,1,2,80]{3,2,1,0:T(2,128)(2,1)} %copy.132), calls=%async_computation.5 | async-start | bytes 1572864 | tf_op jit(solution)/shard_map/all_to_all | solution.py:101
  (11 other events, 24.8 us)
Sparse Core Ops, SparseCore 0:
  9.6 68.3 all-gather.1
  80.2 113.6 reduce-scatter.1
  205.8 63.8 all-reduce.1
where the time goes:
time: 281 us; the launch traced here: 279 us
  waiting for transfers between devices  103 us (37%)
  local copies, waits for them, and re-layouts  67.1 us (24%)
  matrix products  54.1 us (19%)
  starting transfers between devices  33 us (12%)
  between operations  14 us (5%)
  other arithmetic  7.03 us (3%)
    psum x1, waiting for transfers between devices, body(): d_weight = lax.psum(partial_rows, 'seq')  35.8 us
    unnamed x22, local copies, waits for them, and re-layouts  23.1 us
    dot_general x6, matrix products, one_block(): lax.dot_general(probs_low, dout_block, contract_first, preferred_element_...  16.9 us
    all_gather x1, waiting for transfers between devices, body(): lax.all_gather(w_out, 'dp', axis=0, tiled=True)  16.2 us
    while x42, local copies, waits for them, and re-layouts  10.7 us
    all_to_all x1, waiting for transfers between devices, body(): lax.all_to_all(values_heads, 'seq', split_axis=0, concat_axis=1, tiled=True)  10.6 us
    all_to_all x1, waiting for transfers between devices, body(): lax.all_to_all(keys_heads, 'seq', split_axis=0, concat_axis=1, tiled=True)  10.5 us
    dot_general x6, matrix products, one_block(): lax.dot_general(query_block, keys_h, contract_last, preferred_element_typ...  9.55 us
  transfers between devices with their start and end apart: 11, of which 10 were waited for; matrix products, arithmetic and copies ran while one was open for 38% of the time, Pallas kernels for 0%

commit v1 on v0

--- a/solution.py
+++ b/solution.py
@@ -111,7 +111,7 @@
         scatter_dimension=0,
         tiled=True,
     )
-    d_weight = lax.psum(partial_rows, "seq")
+    d_weight = jnp.sum(lax.all_gather(partial_rows, "seq"), axis=0)
     shape_out = (1, tok_rows, features)
     return (
         query_back.reshape(shape_out),

time: 281 us -> 349 us (1.24)
  waiting for transfers between devices: 103 us -> 195 us
  matrix products: 54.1 us -> 40.4 us
  local copies, waits for them, and re-layouts: 67.1 us -> 54.1 us
  other arithmetic: 7.03 us -> 12.2 us
    reduce_scatter x1, waiting for transfers between devices: 0.02 us -> 117 us  [body(): lax.psum_scatter(lax.dot_general(attn_rows, grad_y, contract_first, prefe...]
    psum x1 -> x0, waiting for transfers between devices: 35.8 us -> none  [body(): d_weight = lax.psum(partial_rows, 'seq')]
    dot_general x6, matrix products: 16.9 us -> 4.72 us  [one_block(): lax.dot_general(probs_low, dout_block, contract_first, preferred_element_...]
    while x42 -> x18, local copies, waits for them, and re-layouts: 10.7 us -> 0.05 us
    all_to_all x1, waiting for transfers between devices: 4.46 us -> 14.5 us  [body(): lax.all_to_all(split_heads(d_out), 'seq', split_axis=1, concat_axis=0, ti...]
    reduce_sum x0 -> x1, other arithmetic: none -> 6.92 us  [body(): d_weight = jnp.sum(lax.all_gather(partial_rows, 'seq'), axis=0)]
    unnamed x22 -> x25, local copies, waits for them, and re-layouts: 23.1 us -> 17.5 us
    all_to_all x1, waiting for transfers between devices: 7.23 us -> 1.8 us  [body(): lax.all_to_all(split_heads(keys), 'seq', split_axis=1, concat_axis=0, til...]
  transfers between devices with their start and end apart: 11 -> 11, of which waited for: 10 -> 10; matrix products, arithmetic and copies ran while one was open for 38% -> 24% of each run, Pallas kernels for 0% -> 0%
where the time goes in v1:
time: 349 us; the launch traced here: 347 us
  waiting for transfers between devices  195 us (56%)
  local copies, waits for them, and re-layouts  54.1 us (16%)
  matrix products  40.4 us (12%)
  starting transfers between devices  31.5 us (9%)
  between operations  14.1 us (4%)
  other arithmetic  12.2 us (3%)
    reduce_scatter x1, waiting for transfers between devices, body(): lax.psum_scatter(lax.dot_general(attn_rows, grad_y, contract_first, prefe...  117 us
    unnamed x25, local copies, waits for them, and re-layouts  17.5 us
    all_gather x1, waiting for transfers between devices, body(): lax.all_gather(w_out, 'dp', axis=0, tiled=True)  16.6 us
    all_to_all x1, waiting for transfers between devices, body(): lax.all_to_all(split_heads(d_out), 'seq', split_axis=1, concat_axis=0, ti...  14.5 us
    all_to_all x1, waiting for transfers between devices, body(): lax.all_to_all(keys_heads, 'seq', split_axis=0, concat_axis=1, tiled=True)  10.7 us
    all_to_all x1, waiting for transfers between devices, body(): lax.all_to_all(query_heads, 'seq', split_axis=0, concat_axis=1, tiled=True)  10.5 us
    dot_general x6, matrix products, one_block(): lax.dot_general(query_block, keys_h, contract_last, preferred_element_typ...  9.76 us
    dot_general x6, matrix products, one_block(): lax.dot_general(d_scores, query_block, contract_first, preferred_element_...  8.25 us
  transfers between devices with their start and end apart: 11, of which 10 were waited for; matrix products, arithmetic and copies ran while one was open for 24% of the time, Pallas kernels for 0%

profile of v1, /device:TPU:0, one launch (start us, length us, event | category | flops | bytes accessed | tf_op | source)
XLA Modules:
  0.0 347.3 jit_solution(13246287749584502255)
XLA Ops:
  8.2 4.8 %convolution_multiply_fusion.2 = f32[1280,1280]{1,0:T(8,128)} fusion(bf16[1,192,1280]{2,1,0:T(8,128)(2,1)} %param.13, bf16[1,192,1280]{2,1,0:T(8,128)(2,1)S(1)} %copy-done), kind=kOutput, calls=%fused_computation.54 | convolution fusion | flops 630784000 | bytes 7536640 | tf_op jit(solution)/shard_map/dot_general | solution.py:108
  13.9 117.1 %reduce-scatter.2.cloned.1.call-done = f32[320,1280]{1,0:T(8,128)} async-done(((f32[1280,1280]{1,0:T(8,128)}), f32[320,1280]{1,0:T(8,128)}) %reduce-scatter.2.cloned.1.call-update) | async-done | bytes 1638416 | tf_op jit(solution)/shard_map/reduce_scatter | solution.py:107
  132.1 4.2 %all-to-all-start = ((bf16[192,8,2,80]{0,3,2,1:T(8,128)(2,1)}), bf16[192,8,2,80]{0,3,2,1:T(8,128)(2,1)}, u32[]{:S(2)}, u32[]{:S(2)}) async-start(bf16[192,8,2,80]{0,3,2,1:T(8,128)(2,1)} %bitcast), calls=%async_computation | async-start | bytes 1310720 | tf_op jit(solution)/shard_map/all_to_all | solution.py:76
  140.7 6.7 %all-to-all-done = bf16[192,8,2,80]{0,3,2,1:T(8,128)(2,1)} async-done(((bf16[192,8,2,80]{0,3,2,1:T(8,128)(2,1)}), bf16[192,8,2,80]{0,3,2,1:T(8,128)(2,1)}, u32[]{:S(2)}, u32[]{:S(2)}) %all-to-all-start) | async-done | bytes 491552 | tf_op jit(solution)/shard_map/all_to_all | solution.py:76
  147.4 3.5 %all-to-all-start.1 = ((bf16[192,8,2,80]{0,3,2,1:T(8,128)(2,1)}), bf16[192,8,2,80]{0,3,2,1:T(8,128)(2,1)S(1)}, u32[]{:S(2)}, u32[]{:S(2)}) async-start(bf16[192,8,2,80]{0,3,2,1:T(8,128)(2,1)} %bitcast.194), calls=%async_computation.1 | async-start | bytes 1310720 | tf_op jit(solution)/shard_map/all_to_all | solution.py:77
  153.2 2.4 all_to_all.95
  162.0 4.2 %all-to-all-start.3 = ((bf16[192,8,2,80]{0,3,2,1:T(8,128)(2,1)}), bf16[192,8,2,80]{0,3,2,1:T(8,128)(2,1)}, u32[]{:S(2)}, u32[]{:S(2)}) async-start(bf16[192,8,2,80]{0,3,2,1:T(8,128)(2,1)} %bitcast.13), calls=%async_computation.3 | async-start | bytes 1310720 | tf_op jit(solution)/shard_map/all_to_all | solution.py:78
  169.7 7.7 %all-to-all-done.3 = bf16[192,8,2,80]{0,3,2,1:T(8,128)(2,1)} async-done(((bf16[192,8,2,80]{0,3,2,1:T(8,128)(2,1)}), bf16[192,8,2,80]{0,3,2,1:T(8,128)(2,1)}, u32[]{:S(2)}, u32[]{:S(2)}) %all-to-all-start.3) | async-done | bytes 491552 | tf_op jit(solution)/shard_map/all_to_all | solution.py:78
  179.6 2.4 all_to_all.107
  182.0 16.6 %all-gather.4.cloned.1.call-done = bf16[1280,1280]{1,0:T(8,128)(2,1)} async-done(((bf16[320,1280]{1,0:T(8,128)(2,1)}), bf16[1280,1280]{1,0:T(8,128)(2,1)}) %all-gather.4.cloned.1.call-update) | async-done | bytes 3276816 | tf_op jit(solution)/shard_map/all_gather | solution.py:67
  198.7 3.9 %convolution_convert_fusion.2 = bf16[192,1280]{1,0:T(8,128)(2,1)} fusion(bf16[1280,1280]{1,0:T(8,128)(2,1)} %all-gather.4.cloned.1.call-done, bf16[1,192,1280]{2,1,0:T(8,128)(2,1)S(1)} %copy-done), kind=kOutput, calls=%fused_computation.55 | convolution fusion | flops 629391360 | bytes 4259840 | tf_op jit(solution)/shard_map/dot_general | solution.py:65
  204.7 4.2 %all-to-all-start.2 = ((bf16[192,8,2,80]{0,3,2,1:T(8,128)(2,1)}), bf16[192,8,2,80]{0,3,2,1:T(8,128)(2,1)}, u32[]{:S(2)}, u32[]{:S(2)}) async-start(bf16[192,8,2,80]{0,3,2,1:T(8,128)(2,1)} %bitcast.195), calls=%async_computation.2 | async-start | bytes 1310720 | tf_op jit(solution)/shard_map/all_to_all | solution.py:79
  213.0 14.5 %all-to-all-done.2 = bf16[192,8,2,80]{0,3,2,1:T(8,128)(2,1)} async-done(((bf16[192,8,2,80]{0,3,2,1:T(8,128)(2,1)}), bf16[192,8,2,80]{0,3,2,1:T(8,128)(2,1)}, u32[]{:S(2)}, u32[]{:S(2)}) %all-to-all-start.2) | async-done | bytes 491552 | tf_op jit(solution)/shard_map/all_to_all | solution.py:79
  227.5 4.4 %all-to-all-start.4 = ((bf16[192,8,2,80]{0,3,2,1:T(8,128)(2,1)}), bf16[192,8,2,80]{0,3,2,1:T(8,128)(2,1)}, u32[]{:S(2)}, u32[]{:S(2)}) async-start(bf16[192,8,2,80]{0,3,2,1:T(8,128)(2,1)} %bitcast.192), calls=%async_computation.4 | async-start | bytes 1310720 | tf_op jit(solution)/shard_map/all_to_all | solution.py:80
  234.2 2.4 all_to_all.103
  244.7 17.9 %while.31 = (s32[]{:T(128)}, f32[1536,80]{0,1:T(8,128)S(1)}, f32[1536,80]{0,1:T(8,128)S(1)}, bf16[3,512,80]{1,2,0:T(8,128)(2,1)S(1)}, bf16[3,512,80]{2,1,0:T(8,1...) while((s32[]{:T(128)}, f32[1536,80]{0,1:T(8,128)S(1)}, ...), condition=%wide.region_8.9_spmd.clone, body=%wide.region_5.8_spmd.clone.sunk | while | flops 638328320 | bytes 22894800 | solution.py:49
  263.2 17.8 %while.30 = (s32[]{:T(128)}, f32[1536,80]{0,1:T(8,128)S(1)}, f32[1536,80]{0,1:T(8,128)S(1)}, bf16[3,512,80]{1,2,0:T(8,128)(2,1)S(1)}, bf16[3,512,80]{2,1,0:T(8,1...) while((s32[]{:T(128)}, f32[1536,80]{0,1:T(8,128)S(1)}, ...), condition=%wide.region_4.5_spmd.clone, body=%wide.region_1.4_spmd.clone.sunk | while | flops 638328320 | bytes 21911732 | solution.py:49
  283.4 3.5 %all-to-all-start.5 = ((bf16[1536,1,2,80]{3,2,1,0:T(2,128)(2,1)}), bf16[1536,1,2,80]{3,2,1,0:T(2,128)(2,1)S(1)}, u32[]{:S(2)}, u32[]{:S(2)}) async-start(bf16[1536,1,2,80]{3,2,1,0:T(2,128)(2,1)} %copy.132), calls=%async_computation.5 | async-start | bytes 1572864 | tf_op jit(solution)/shard_map/all_to_all | solution.py:101
  288.9 10.5 %all-to-all-done.5 = bf16[1536,1,2,80]{3,2,1,0:T(2,128)(2,1)S(1)} async-done(((bf16[1536,1,2,80]{3,2,1,0:T(2,128)(2,1)}), bf16[1536,1,2,80]{3,2,1,0:T(2,128)(2,1)S(1)}, u32[]{:S(2)}, u32[]{:S(2)}) %all-to-all-start.5) | async-done | bytes 491552 | tf_op jit(solution)/shard_map/all_to_all | solution.py:101
  299.5 3.5 %all-to-all-start.6 = ((bf16[1536,1,2,80]{3,2,1,0:T(2,128)(2,1)}), bf16[1536,1,2,80]{3,2,1,0:T(2,128)(2,1)S(1)}, u32[]{:S(2)}, u32[]{:S(2)}) async-start(bf16[1536,1,2,80]{3,2,1,0:T(2,128)(2,1)} %copy.135), calls=%async_computation.6 | async-start | bytes 1572864 | tf_op jit(solution)/shard_map/all_to_all | solution.py:102
  304.9 10.7 %all-to-all-done.6 = bf16[1536,1,2,80]{3,2,1,0:T(2,128)(2,1)S(1)} async-done(((bf16[1536,1,2,80]{3,2,1,0:T(2,128)(2,1)}), bf16[1536,1,2,80]{3,2,1,0:T(2,128)(2,1)S(1)}, u32[]{:S(2)}, u32[]{:S(2)}) %all-to-all-start.6) | async-done | bytes 491552 | tf_op jit(solution)/shard_map/all_to_all | solution.py:102
  315.5 3.8 %all-to-all-start.7 = ((bf16[1536,1,2,80]{3,2,1,0:T(2,128)(2,1)}), bf16[1536,1,2,80]{3,2,1,0:T(2,128)(2,1)S(1)}, u32[]{:S(2)}, u32[]{:S(2)}) async-start(bf16[1536,1,2,80]{3,2,1,0:T(2,128)(2,1)} %copy.137), calls=%async_computation.7 | async-start | bytes 1572864 | tf_op jit(solution)/shard_map/all_to_all | solution.py:103
  325.2 6.4 %all-to-all-done.7 = bf16[1536,1,2,80]{3,2,1,0:T(2,128)(2,1)S(1)} async-done(((bf16[1536,1,2,80]{3,2,1,0:T(2,128)(2,1)}), bf16[1536,1,2,80]{3,2,1,0:T(2,128)(2,1)S(1)}, u32[]{:S(2)}, u32[]{:S(2)}) %all-to-all-start.7) | async-done | bytes 491552 | tf_op jit(solution)/shard_map/all_to_all | solution.py:103
  333.9 6.9 %reduce_sum.40 = f32[320,1280]{1,0:T(8,128)} reduce(f32[8,320,1280]{2,1,0:T(8,128)} %bitcast.184, f32[]{:T(128)} %constant.39.clone.1), dimensions={0}, to_apply=%region_10.11 | reduce | flops 2867200 | bytes 14745604 | tf_op jit(solution)/shard_map/reduce_sum | solution.py:114
  (138 shorter events, 88.4 us)
Async XLA Ops:
  7.2 123.8 %reduce-scatter.2.cloned.1.call-start = ((), (), s32[]{:S(2)}) async-start(), calls=%async_computation.10 | async-start | bytes 8192000 | tf_op jit(solution)/shard_map/reduce_scatter | solution.py:107
  13.0 118.0 %copy-start.6 = (bf16[1,192,1280]{2,1,0:T(8,128)(2,1)S(1)}, bf16[1,192,1280]{2,1,0:T(8,128)(2,1)}, u32[]{:S(2)}) copy-start(bf16[1,192,1280]{2,1,0:T(8,128)(2,1)} %param.10) | copy-start | bytes 1474564
  13.0 123.3 %copy-start.5 = (bf16[1,192,1280]{2,1,0:T(8,128)(2,1)S(1)}, bf16[1,192,1280]{2,1,0:T(8,128)(2,1)}, u32[]{:S(2)}) copy-start(bf16[1,192,1280]{2,1,0:T(8,128)(2,1)} %param.13) | copy-start | bytes 1474564
  13.1 124.4 %copy-start.7 = (bf16[1,192,1280]{2,1,0:T(8,128)(2,1)S(1)}, bf16[1,192,1280]{2,1,0:T(8,128)(2,1)}, u32[]{:S(2)}) copy-start(bf16[1,192,1280]{2,1,0:T(8,128)(2,1)} %param.11) | copy-start | bytes 1474564
  13.1 185.6 %all-gather.4.cloned.1.call-start = ((), (), s32[]{:S(2)}) async-start(), calls=%async_computation.9 | async-start | bytes 4096000 | tf_op jit(solution)/shard_map/all_gather | solution.py:67
  13.8 320.1 %all-gather.6.cloned.1.call-start = ((), (), s32[]{:S(2)}) async-start(), calls=%async_computation.11 | async-start | bytes 14745600 | tf_op jit(solution)/shard_map/all_gather | solution.py:114
  132.1 15.3 %all-to-all-start = ((bf16[192,8,2,80]{0,3,2,1:T(8,128)(2,1)}), bf16[192,8,2,80]{0,3,2,1:T(8,128)(2,1)}, u32[]{:S(2)}, u32[]{:S(2)}) async-start(bf16[192,8,2,80]{0,3,2,1:T(8,128)(2,1)} %bitcast), calls=%async_computation | async-start | bytes 1310720 | tf_op jit(solution)/shard_map/all_to_all | solution.py:76
  147.4 14.6 %all-to-all-start.1 = ((bf16[192,8,2,80]{0,3,2,1:T(8,128)(2,1)}), bf16[192,8,2,80]{0,3,2,1:T(8,128)(2,1)S(1)}, u32[]{:S(2)}, u32[]{:S(2)}) async-start(bf16[192,8,2,80]{0,3,2,1:T(8,128)(2,1)} %bitcast.194), calls=%async_computation.1 | async-start | bytes 1310720 | tf_op jit(solution)/shard_map/all_to_all | solution.py:77
  162.0 15.3 %all-to-all-start.3 = ((bf16[192,8,2,80]{0,3,2,1:T(8,128)(2,1)}), bf16[192,8,2,80]{0,3,2,1:T(8,128)(2,1)}, u32[]{:S(2)}, u32[]{:S(2)}) async-start(bf16[192,8,2,80]{0,3,2,1:T(8,128)(2,1)} %bitcast.13), calls=%async_computation.3 | async-start | bytes 1310720 | tf_op jit(solution)/shard_map/all_to_all | solution.py:78
  204.7 22.8 %all-to-all-start.2 = ((bf16[192,8,2,80]{0,3,2,1:T(8,128)(2,1)}), bf16[192,8,2,80]{0,3,2,1:T(8,128)(2,1)}, u32[]{:S(2)}, u32[]{:S(2)}) async-start(bf16[192,8,2,80]{0,3,2,1:T(8,128)(2,1)} %bitcast.195), calls=%async_computation.2 | async-start | bytes 1310720 | tf_op jit(solution)/shard_map/all_to_all | solution.py:79
  227.5 15.5 %all-to-all-start.4 = ((bf16[192,8,2,80]{0,3,2,1:T(8,128)(2,1)}), bf16[192,8,2,80]{0,3,2,1:T(8,128)(2,1)}, u32[]{:S(2)}, u32[]{:S(2)}) async-start(bf16[192,8,2,80]{0,3,2,1:T(8,128)(2,1)} %bitcast.192), calls=%async_computation.4 | async-start | bytes 1310720 | tf_op jit(solution)/shard_map/all_to_all | solution.py:80
  244.7 2.3 copy-start.4
  246.4 1.4 copy-start.2
  250.7 2.2 copy-start.4
  252.4 1.4 copy-start.2
  256.7 2.2 copy-start.4
  258.3 1.4 copy-start.2
  263.2 2.2 copy-start.3
  269.2 2.2 copy-start.3
  275.1 2.2 copy-start.3
  283.4 16.1 %all-to-all-start.5 = ((bf16[1536,1,2,80]{3,2,1,0:T(2,128)(2,1)}), bf16[1536,1,2,80]{3,2,1,0:T(2,128)(2,1)S(1)}, u32[]{:S(2)}, u32[]{:S(2)}) async-start(bf16[1536,1,2,80]{3,2,1,0:T(2,128)(2,1)} %copy.132), calls=%async_computation.5 | async-start | bytes 1572864 | tf_op jit(solution)/shard_map/all_to_all | solution.py:101
  299.5 16.1 %all-to-all-start.6 = ((bf16[1536,1,2,80]{3,2,1,0:T(2,128)(2,1)}), bf16[1536,1,2,80]{3,2,1,0:T(2,128)(2,1)S(1)}, u32[]{:S(2)}, u32[]{:S(2)}) async-start(bf16[1536,1,2,80]{3,2,1,0:T(2,128)(2,1)} %copy.135), calls=%async_computation.6 | async-start | bytes 1572864 | tf_op jit(solution)/shard_map/all_to_all | solution.py:102
  315.5 16.1 %all-to-all-start.7 = ((bf16[1536,1,2,80]{3,2,1,0:T(2,128)(2,1)}), bf16[1536,1,2,80]{3,2,1,0:T(2,128)(2,1)S(1)}, u32[]{:S(2)}, u32[]{:S(2)}) async-start(bf16[1536,1,2,80]{3,2,1,0:T(2,128)(2,1)} %copy.137), calls=%async_computation.7 | async-start | bytes 1572864 | tf_op jit(solution)/shard_map/all_to_all | solution.py:103
  333.9 6.9 %copy-start.1 = (bf16[1,192,1280]{2,1,0:T(8,128)(2,1)S(1)}, bf16[1,192,1280]{2,1,0:T(8,128)(2,1)}, u32[]{:S(2)}) copy-start(bf16[1,192,1280]{2,1,0:T(8,128)(2,1)} %param.14) | copy-start | bytes 1474564
  (1 other events, 1.0 us)
Sparse Core Ops, SparseCore 0:
  13.2 117.7 reduce-scatter.1
  132.5 66.0 all-gather.3
  200.6 84.2 all-gather.5
